TPU v7x, 512 devices: a whole 4x8x8 slice. The times are simulated.
512 devices in a mesh: gx: 64 (over y, x, core), gz: 8 (over z).
Axes of the slice: x: 4, y: 8, z: 8, core: 2. Of those that a mesh axis runs over, the one named last changes fastest.
Arguments:
- velocity: bfloat16 [3, 32, 512, 64, 128], P(None, None, 'gx', 'gz'), may hold values from -16 to 16
- weights: float32 [512, 64, 128], P('gx', 'gz'), may hold values from 1 to 60
Outputs:
- modes: float32 [3, 32, 512, 64, 128], P(None, None, 'gx', 'gz')
All inputs are finite; a program needn't handle non-finite values.
Results may differ from a plain program's by a relative error of at most 0.0003.
Values may be sent and summed in bfloat16 or wider, within the bound.
A program may use at most 64 MiB of HBM per device.

v0:
```python
import jax
import jax.numpy as jnp
from jax import lax
from jax.sharding import PartitionSpec as P

COEFS = (0.8, -0.2, 4.0 / 105.0, -1.0 / 280.0)


def extended_2(cells, sides, width):
    for axis, dim in sides:
        count = lax.axis_size(axis)
        head = lax.slice_in_dim(cells, 0, width, axis=dim)
        tail = lax.slice_in_dim(cells, cells.shape[dim] - width, cells.shape[dim], axis=dim)
        cells = jnp.concatenate(
            [
                lax.ppermute(tail, axis, [(i, (i + 1) % count) for i in range(count)]),
                cells,
                lax.ppermute(head, axis, [((i + 1) % count, i) for i in range(count)]),
            ],
            axis=dim,
        )
    return cells


def taps(extended, axis, length):
    total = None
    for step, weight in enumerate(COEFS, start=1):
        upper = lax.slice_in_dim(extended, 4 + step, 4 + step + length, axis=axis)
        lower = lax.slice_in_dim(extended, 4 - step, 4 - step + length, axis=axis)
        term = weight * (upper - lower)
        total = term if total is None else total + term
    return total


def walled(field):
    padded = jnp.pad(field, ((0, 0), (0, 0), (0, 0), (4, 4)))
    return taps(padded, 3, field.shape[3])


def per_device(velocity, weights):
    snaps = velocity.shape[1]
    cells_x = velocity.shape[2]
    cells_z = velocity.shape[3]
    cells_y = velocity.shape[4]
    whole_ext = extended_2(velocity, (("gx", 2), ("gz", 3)), 4)
    v_stream = whole_ext[1, :, :, 4 : 4 + cells_z].astype(jnp.float32)
    w_stream = whole_ext[2, :, :, 4 : 4 + cells_z].astype(jnp.float32)
    u_span = whole_ext[0, :, 4 : 4 + cells_x].astype(jnp.float32)
    v_span = whole_ext[1, :, 4 : 4 + cells_x].astype(jnp.float32)
    inner_u = velocity[0].astype(jnp.float32)
    inner_w = velocity[2].astype(jnp.float32)
    omega_x = walled(inner_w) - taps(v_span, 2, cells_z)
    omega_y = taps(u_span, 2, cells_z) - taps(w_stream, 1, cells_x)
    omega_z = taps(v_stream, 1, cells_x) - walled(inner_u)
    vort = jnp.stack([omega_x, omega_y, omega_z])
    local_gram = lax.dot_general(
        vort * weights[None, None],
        vort,
        (((0, 2, 3, 4), (0, 2, 3, 4)), ((), ())),
        precision=lax.Precision.HIGHEST,
        preferred_element_type=jnp.float32,
    )
    factor = jnp.linalg.cholesky(lax.psum(local_gram, ("gx", "gz")))
    inverse = jax.scipy.linalg.solve_triangular(
        factor, jnp.eye(snaps, dtype=jnp.float32), lower=True
    )
    rows_all = 3 * cells_x * cells_y * cells_z * lax.axis_size("gx") * lax.axis_size("gz")
    scale_all = jnp.sqrt(jnp.float32(rows_all))
    mixed = jnp.einsum("ij,cjxzy->cixzy", inverse, vort, precision=lax.Precision.HIGHEST)
    return mixed * scale_all


def solution(mesh):
    placed = (P(None, None, "gx", "gz", None), P("gx", "gz", None))
    return jax.shard_map(
        per_device,
        mesh=mesh,
        in_specs=placed,
        out_specs=P(None, None, "gx", "gz", None),
        check_vma=False,
    )
```

profile of v0, /device:TPU:1, one launch (start us, length us, event | category | flops | bytes accessed | tf_op | source)
XLA Modules:
  0.0 188.6 jit_solution(6746897384506120188)
XLA Ops:
  0.0 2.4 %copy.3 = bf16[3,32,8,8,128]{4,1,3,2,0:T(8,128)(2,1)S(1)} copy(bf16[3,32,8,8,128]{4,3,2,1,0:T(8,128)(2,1)} %param.2) | data formatting | bytes 3145728 | tf_op args[0]
  2.8 4.6 %collective-permute-start = (bf16[3,32,4,8,128]{4,1,3,2,0:T(8,128)(2,1)S(1)}, bf16[3,32,4,8,128]{4,1,3,2,0:T(8,128)(2,1)S(1)}, u32[]{:S(2)}, u32[]{:S(2)}) collective-permute-start(bf16[3,32,4,8,128]{4,1,3,2,0:T(8,128)(2,1)S(1)} %get-tuple-element.14), channel_id=1, source_target_pairs={{0,8},{8,16},{16,24},{24,32},{32,40},{40,48},{48,56},{56,64},{64,7... | collective-permute-start | bytes 2359304 | tf_op jit(solution)/shard_map/ppermute | solution.py:16
  7.4 6.2 %collective-permute-start.1 = (bf16[3,32,4,8,128]{4,1,3,2,0:T(8,128)(2,1)S(1)}, bf16[3,32,4,8,128]{4,1,3,2,0:T(8,128)(2,1)S(1)}, u32[]{:S(2)}, u32[]{:S(2)}) collective-permute-start(bf16[3,32,4,8,128]{4,1,3,2,0:T(8,128)(2,1)S(1)} %get-tuple-element.13), channel_id=1, source_target_pairs={{8,0},{16,8},{24,16},{32,24},{40,32},{48,40},{56,48},{64,56},{72,6... | collective-permute-start | bytes 2359304 | tf_op jit(solution)/shard_map/ppermute | solution.py:18
  13.6 2.7 %collective-permute-done = bf16[3,32,4,8,128]{4,1,3,2,0:T(8,128)(2,1)S(1)} collective-permute-done((bf16[3,32,4,8,128]{4,1,3,2,0:T(8,128)(2,1)S(1)}, bf16[3,32,4,8,128]{4,1,3,2,0:T(8,128)(2,1)S(1)}, u32[]{:S(2)}, u32[]{:S(2)}) %collective-permute-start) | collective-permute-done | bytes 786464 | tf_op jit(solution)/shard_map/ppermute | solution.py:16
  16.4 1.1 constant_dynamic-update-slice_fusion.1
  17.5 3.5 %collective-permute-done.1 = bf16[3,32,4,8,128]{4,1,3,2,0:T(8,128)(2,1)S(1)} collective-permute-done((bf16[3,32,4,8,128]{4,1,3,2,0:T(8,128)(2,1)S(1)}, bf16[3,32,4,8,128]{4,1,3,2,0:T(8,128)(2,1)S(1)}, u32[]{:S(2)}, u32[]{:S(2)}) %collective-permute-start.1) | collective-permute-done | bytes 786464 | tf_op jit(solution)/shard_map/ppermute | solution.py:18
  21.1 1.0 fusion.65
  22.2 3.7 %collective-permute-start.2 = (bf16[3,32,16,4,128]{4,1,3,2,0:T(8,128)(2,1)S(1)}, bf16[3,32,16,4,128]{4,1,3,2,0:T(8,128)(2,1)S(1)}, u32[]{:S(2)}, u32[]{:S(2)}) collective-permute-start(bf16[3,32,16,4,128]{4,1,3,2,0:T(8,128)(2,1)S(1)} %get-tuple-element.7), channel_id=1, source_target_pairs={{0,1},{1,2},{2,3},{3,4},{4,5},{5,6},{6,7},{7,0},{8,9},{9,10},{10,1... | collective-permute-start | bytes 4718600 | tf_op jit(solution)/shard_map/ppermute | solution.py:16
  25.9 8.6 %collective-permute-start.3 = (bf16[3,32,16,4,128]{4,1,3,2,0:T(8,128)(2,1)S(1)}, bf16[3,32,16,4,128]{4,1,3,2,0:T(8,128)(2,1)S(1)}, u32[]{:S(2)}, u32[]{:S(2)}) collective-permute-start(bf16[3,32,16,4,128]{4,1,3,2,0:T(8,128)(2,1)S(1)} %get-tuple-element.8), channel_id=1, source_target_pairs={{1,0},{2,1},{3,2},{4,3},{5,4},{6,5},{7,6},{0,7},{9,8},{10,9},{11,1... | collective-permute-start | bytes 4718600 | tf_op jit(solution)/shard_map/ppermute | solution.py:18
  34.6 0.7 pad_convert_fusion
  35.3 0.6 fusion.33
  35.9 2.1 %fusion.10 = f32[1,32,8,8,128]{4,1,3,2,0:T(8,128)S(1)} fusion(f32[32,8,8,136]{3,0,2,1:T(8,128)S(1)} %get-tuple-element.15, f32[32,16,8,128]{3,0,2,1:T(8,128)S(1)} %get-tuple-element.10), kind=kLoop, calls=%fused_computation.12 | loop fusion | flops 6029312 | bytes 17825792 | tf_op jit(solution)/shard_map/stack | solution.py:55
  37.9 27.2 %collective-permute-done.2 = bf16[3,32,16,4,128]{4,1,3,2,0:T(8,128)(2,1)S(1)} collective-permute-done((bf16[3,32,16,4,128]{4,1,3,2,0:T(8,128)(2,1)S(1)}, bf16[3,32,16,4,128]{4,1,3,2,0:T(8,128)(2,1)S(1)}, u32[]{:S(2)}, u32[]{:S(2)}) %collective-permute-start.2) | collective-permute-done | bytes 1572896 | tf_op jit(solution)/shard_map/ppermute | solution.py:16
  65.1 0.9 collective-permute-done.3
  66.4 2.1 %fusion.27 = f32[1,32,8,8,128]{4,1,3,2,0:T(8,128)S(1)} fusion(f32[32,16,8,128]{3,0,2,1:T(8,128)S(1)} %get-tuple-element.9, f32[32,8,16,128]{3,0,2,1:T(8,128)S(1)} %get-tuple-element.6), kind=kLoop, calls=%fused_computation.38 | loop fusion | flops 6029312 | bytes 17825792 | tf_op jit(solution)/shard_map/stack | solution.py:55
  68.5 2.1 %fusion.46 = f32[1,32,8,8,128]{4,1,3,2,0:T(8,128)S(1)} fusion(f32[32,8,16,128]{3,0,2,1:T(8,128)S(1)} %get-tuple-element.5, f32[32,8,8,136]{3,0,2,1:T(8,128)S(1)} %get-tuple-element.16), kind=kLoop, calls=%fused_computation.68 | loop fusion | flops 6029312 | bytes 17825792 | tf_op jit(solution)/shard_map/stack | solution.py:55
  70.6 2.8 %fusion.4 = f32[32,32]{0,1:T(8,128)S(1)} fusion(f32[1,32,8,8,128]{4,1,3,2,0:T(8,128)S(1)} %fusion.10, f32[1,32,8,8,128]{4,1,3,2,0:T(8,128)S(1)} %fusion.27, f32[1,32,8,8,128]{4,1,3,2,0:T(8,128)S(1)} %fusion.46, f32[8,8,128]{2,1,0:T(8,128)S(1)} %copy-done.1), kind=kOutput, calls=%fused_computation.6 | convolution fusion | flops 305922048 | bytes 3182592 | tf_op jit(solution)/shard_map/dot_general | solution.py:56
  73.4 101.7 %psum.7 = f32[32,32]{0,1:T(8,128)S(1)} all-reduce(f32[32,32]{0,1:T(8,128)S(1)} %fusion.4), channel_id=1, replica_groups=mesh['gx'=64,'gz'=8] {'gx','gz'}, use_global_device_ids=true, to_apply=%region_0.1 | all-reduce | flops 1024 | bytes 8192 | tf_op jit(solution)/shard_map/psum | solution.py:63
  175.2 2.9 %cholesky.17 = f32[32,32]{1,0:T(8,128)S(1)} custom-call(f32[32,32]{1,0:T(8,128)S(1)} %fusion.62), custom_call_target="Cholesky" | custom-call | tf_op jit(solution)/shard_map/jit(cholesky)/cholesky | solution.py:63
  178.2 0.6 compare_reduce_fusion
  178.8 0.7 fusion.60
  179.5 2.4 %custom-call.7 = f32[1,32,32]{1,2,0:T(8,128)S(1)} custom-call(f32[1,32,32]{2,1,0:T(8,128)S(1)} %fusion.60), custom_call_target="InvertDiagBlocksLowerTriangular" | custom-call | tf_op jit(solution)/shard_map/jit(_solve_triangular)/triangular_solve | solution.py:64
  182.1 3.0 %multiply_bitcast_fusion = f32[3,32,8,8,128]{4,1,3,2,0:T(8,128)S(1)} fusion(f32[32,32,1,1,1]{1,0,4,3,2:T(8,128)S(1)} %convolution_bitcast_fusion, f32[1,32,8,8,128]{4,1,3,2,0:T(8,128)S(1)} %fusion.10, f32[1,32,8,8,128]{4,1,3,2,0:T(8,128)S(1)} %fusion.27, f32[1,32,8,8,128]{4,1,3,2,0:T(8,128)S(1)} %fusion.46), kind=kOutput, calls=%fused_computation.3 | convolution fusion | flops 304349184 | bytes 6295552 | tf_op jit(solution)/shard_map/ij,cjxzy->cixzy/dot_general | solution.py:69
  185.1 3.5 %copy.10 = f32[3,32,8,8,128]{4,3,2,1,0:T(8,128)} copy(f32[3,32,8,8,128]{4,1,3,2,0:T(8,128)S(1)} %multiply_bitcast_fusion) | data formatting | bytes 6291456 | tf_op jit(solution)/shard_map/mul | solution.py:70
  (13 shorter events, 1.2 us)
Async XLA Ops:
  2.4 14.0 %copy-start = (bf16[3,32,8,8,128]{4,3,2,1,0:T(8,128)(2,1)S(1)}, bf16[3,32,8,8,128]{4,3,2,1,0:T(8,128)(2,1)}, u32[]{:S(2)}) copy-start(bf16[3,32,8,8,128]{4,3,2,1,0:T(8,128)(2,1)} %param.2) | copy-start | bytes 4718596
  2.8 13.6 %collective-permute-start = (bf16[3,32,4,8,128]{4,1,3,2,0:T(8,128)(2,1)S(1)}, bf16[3,32,4,8,128]{4,1,3,2,0:T(8,128)(2,1)S(1)}, u32[]{:S(2)}, u32[]{:S(2)}) collective-permute-start(bf16[3,32,4,8,128]{4,1,3,2,0:T(8,128)(2,1)S(1)} %get-tuple-element.14), channel_id=1, source_target_pairs={{0,8},{8,16},{16,24},{24,32},{32,40},{40,48},{48,56},{56,64},{64,7... | collective-permute-start | bytes 2359304 | tf_op jit(solution)/shard_map/ppermute | solution.py:16
  7.4 13.6 %collective-permute-start.1 = (bf16[3,32,4,8,128]{4,1,3,2,0:T(8,128)(2,1)S(1)}, bf16[3,32,4,8,128]{4,1,3,2,0:T(8,128)(2,1)S(1)}, u32[]{:S(2)}, u32[]{:S(2)}) collective-permute-start(bf16[3,32,4,8,128]{4,1,3,2,0:T(8,128)(2,1)S(1)} %get-tuple-element.13), channel_id=1, source_target_pairs={{8,0},{16,8},{24,16},{32,24},{40,32},{48,40},{56,48},{64,56},{72,6... | collective-permute-start | bytes 2359304 | tf_op jit(solution)/shard_map/ppermute | solution.py:18
  22.2 43.0 %collective-permute-start.2 = (bf16[3,32,16,4,128]{4,1,3,2,0:T(8,128)(2,1)S(1)}, bf16[3,32,16,4,128]{4,1,3,2,0:T(8,128)(2,1)S(1)}, u32[]{:S(2)}, u32[]{:S(2)}) collective-permute-start(bf16[3,32,16,4,128]{4,1,3,2,0:T(8,128)(2,1)S(1)} %get-tuple-element.7), channel_id=1, source_target_pairs={{0,1},{1,2},{2,3},{3,4},{4,5},{5,6},{6,7},{7,0},{8,9},{9,10},{10,1... | collective-permute-start | bytes 4718600 | tf_op jit(solution)/shard_map/ppermute | solution.py:16
  25.9 40.1 %collective-permute-start.3 = (bf16[3,32,16,4,128]{4,1,3,2,0:T(8,128)(2,1)S(1)}, bf16[3,32,16,4,128]{4,1,3,2,0:T(8,128)(2,1)S(1)}, u32[]{:S(2)}, u32[]{:S(2)}) collective-permute-start(bf16[3,32,16,4,128]{4,1,3,2,0:T(8,128)(2,1)S(1)} %get-tuple-element.8), channel_id=1, source_target_pairs={{1,0},{2,1},{3,2},{4,3},{5,4},{6,5},{7,6},{0,7},{9,8},{10,9},{11,1... | collective-permute-start | bytes 4718600 | tf_op jit(solution)/shard_map/ppermute | solution.py:18
  68.5 2.1 %copy-start.1 = (f32[8,8,128]{2,1,0:T(8,128)S(1)}, f32[8,8,128]{2,1,0:T(8,128)}, u32[]{:S(2)}) copy-start(f32[8,8,128]{2,1,0:T(8,128)} %param.3) | copy-start | bytes 98308
where the time goes:
time: 189 us
  blocking collectives  102 us (54%)
  waiting for transfers between devices  34.3 us (18%)
  starting transfers between devices  23.1 us (12%)
  other arithmetic  14.6 us (8%)
  local copies, waits for them, and re-layouts  8.7 us (5%)
  matrix products  6.01 us (3%)
    psum x1, blocking collectives, per_device(): factor = jnp.linalg.cholesky(lax.psum(local_gram, ('gx', 'gz')))  102 us
    ppermute x2, waiting for transfers between devices, extended_2(): lax.ppermute(tail, axis, [(i, (i + 1) % count) for i in range(count)])  29.9 us
    ppermute x2, starting transfers between devices, extended_2(): lax.ppermute(head, axis, [((i + 1) % count, i) for i in range(count)])  14.8 us
    ppermute x2, starting transfers between devices, extended_2(): lax.ppermute(tail, axis, [(i, (i + 1) % count) for i in range(count)])  8.35 us
    another operation x3, other arithmetic, per_device(): vort = jnp.stack([omega_x, omega_y, omega_z])  6.27 us
    ppermute x2, waiting for transfers between devices, extended_2(): lax.ppermute(head, axis, [((i + 1) % count, i) for i in range(count)])  4.41 us
  transfers between devices with their start and end apart: 4, of which 4 were waited for; matrix products, arithmetic and copies ran while one was open for 2% of the time, Pallas kernels for 0%

commit v1 on v0

--- a/solution.py
+++ b/solution.py
@@ -60,7 +60,7 @@
         precision=lax.Precision.HIGHEST,
         preferred_element_type=jnp.float32,
     )
-    factor = jnp.linalg.cholesky(lax.psum(local_gram, ("gx", "gz")))
+    factor = jnp.linalg.cholesky(jnp.sum(lax.all_gather(local_gram, ("gx", "gz")), axis=0))
     inverse = jax.scipy.linalg.solve_triangular(
         factor, jnp.eye(snaps, dtype=jnp.float32), lower=True
     )

time: 189 us -> 235 us (1.24)
  waiting for transfers between devices: 34.3 us -> 164 us
  blocking collectives: 102 us -> 0 us
  between operations: 0.18 us -> 13.6 us
  other arithmetic: 14.6 us -> 18.7 us
    all_gather x0 -> x1, waiting for transfers between devices: none -> 130 us  [per_device(): lax.all_gather(local_gram, ('gx', 'gz'))]
    psum x1 -> x0, blocking collectives: 102 us -> none  [per_device(): factor = jnp.linalg.cholesky(lax.psum(local_gram, ('gx', 'gz')))]
    reduce_sum x0 -> x1, other arithmetic: none -> 3.99 us  [per_device(): jnp.sum(lax.all_gather(local_gram, ('gx', 'gz')), axis=0)]
  transfers between devices with their start and end apart: 4 -> 5, of which waited for: 4 -> 5; matrix products, arithmetic and copies ran while one was open for 2% -> 2% of each run, Pallas kernels for 0% -> 0%
where the time goes in v1:
time: 235 us
  waiting for transfers between devices  164 us (70%)
  starting transfers between devices  23.1 us (10%)
  other arithmetic  18.7 us (8%)
  between operations  13.6 us (6%)
  local copies, waits for them, and re-layouts  8.7 us (4%)
  matrix products  6.57 us (3%)
    all_gather x1, waiting for transfers between devices, per_device(): lax.all_gather(local_gram, ('gx', 'gz'))  130 us
    ppermute x2, waiting for transfers between devices, extended_2(): lax.ppermute(tail, axis, [(i, (i + 1) % count) for i in range(count)])  29.9 us
    ppermute x2, starting transfers between devices, extended_2(): lax.ppermute(head, axis, [((i + 1) % count, i) for i in range(count)])  14.8 us
    ppermute x2, starting transfers between devices, extended_2(): lax.ppermute(tail, axis, [(i, (i + 1) % count) for i in range(count)])  8.35 us
    another operation x3, other arithmetic, per_device(): vort = jnp.stack([omega_x, omega_y, omega_z])  6.45 us
  transfers between devices with their start and end apart: 5, of which 5 were waited for; matrix products, arithmetic and copies ran while one was open for 2% of the time, Pallas kernels for 0%

profile of v1, /device:TPU:1, one launch (start us, length us, event | category | flops | bytes accessed | tf_op | source)
XLA Modules:
  0.0 234.6 jit_solution(14224738332593391067)
XLA Ops:
  6.5 2.4 %copy.10 = bf16[3,32,8,8,128]{4,1,3,2,0:T(8,128)(2,1)S(1)} copy(bf16[3,32,8,8,128]{4,3,2,1,0:T(8,128)(2,1)} %param.2) | data formatting | bytes 3145728 | tf_op args[0]
  9.3 4.6 %collective-permute-start = (bf16[3,32,4,8,128]{4,1,3,2,0:T(8,128)(2,1)S(1)}, bf16[3,32,4,8,128]{4,1,3,2,0:T(8,128)(2,1)S(1)}, u32[]{:S(2)}, u32[]{:S(2)}) collective-permute-start(bf16[3,32,4,8,128]{4,1,3,2,0:T(8,128)(2,1)S(1)} %get-tuple-element.14), channel_id=1, source_target_pairs={{0,8},{8,16},{16,24},{24,32},{32,40},{40,48},{48,56},{56,64},{64,7... | collective-permute-start | bytes 2359304 | tf_op jit(solution)/shard_map/ppermute | solution.py:16
  14.0 6.2 %collective-permute-start.1 = (bf16[3,32,4,8,128]{4,1,3,2,0:T(8,128)(2,1)S(1)}, bf16[3,32,4,8,128]{4,1,3,2,0:T(8,128)(2,1)S(1)}, u32[]{:S(2)}, u32[]{:S(2)}) collective-permute-start(bf16[3,32,4,8,128]{4,1,3,2,0:T(8,128)(2,1)S(1)} %get-tuple-element.13), channel_id=1, source_target_pairs={{8,0},{16,8},{24,16},{32,24},{40,32},{48,40},{56,48},{64,56},{72,6... | collective-permute-start | bytes 2359304 | tf_op jit(solution)/shard_map/ppermute | solution.py:18
  20.2 2.7 %collective-permute-done = bf16[3,32,4,8,128]{4,1,3,2,0:T(8,128)(2,1)S(1)} collective-permute-done((bf16[3,32,4,8,128]{4,1,3,2,0:T(8,128)(2,1)S(1)}, bf16[3,32,4,8,128]{4,1,3,2,0:T(8,128)(2,1)S(1)}, u32[]{:S(2)}, u32[]{:S(2)}) %collective-permute-start) | collective-permute-done | bytes 786464 | tf_op jit(solution)/shard_map/ppermute | solution.py:16
  22.9 1.1 constant_dynamic-update-slice_fusion.1
  24.1 3.5 %collective-permute-done.1 = bf16[3,32,4,8,128]{4,1,3,2,0:T(8,128)(2,1)S(1)} collective-permute-done((bf16[3,32,4,8,128]{4,1,3,2,0:T(8,128)(2,1)S(1)}, bf16[3,32,4,8,128]{4,1,3,2,0:T(8,128)(2,1)S(1)}, u32[]{:S(2)}, u32[]{:S(2)}) %collective-permute-start.1) | collective-permute-done | bytes 786464 | tf_op jit(solution)/shard_map/ppermute | solution.py:18
  27.7 1.0 fusion.65
  28.7 3.7 %collective-permute-start.2 = (bf16[3,32,16,4,128]{4,1,3,2,0:T(8,128)(2,1)S(1)}, bf16[3,32,16,4,128]{4,1,3,2,0:T(8,128)(2,1)S(1)}, u32[]{:S(2)}, u32[]{:S(2)}) collective-permute-start(bf16[3,32,16,4,128]{4,1,3,2,0:T(8,128)(2,1)S(1)} %get-tuple-element.7), channel_id=1, source_target_pairs={{0,1},{1,2},{2,3},{3,4},{4,5},{5,6},{6,7},{7,0},{8,9},{9,10},{10,1... | collective-permute-start | bytes 4718600 | tf_op jit(solution)/shard_map/ppermute | solution.py:16
  32.4 8.6 %collective-permute-start.3 = (bf16[3,32,16,4,128]{4,1,3,2,0:T(8,128)(2,1)S(1)}, bf16[3,32,16,4,128]{4,1,3,2,0:T(8,128)(2,1)S(1)}, u32[]{:S(2)}, u32[]{:S(2)}) collective-permute-start(bf16[3,32,16,4,128]{4,1,3,2,0:T(8,128)(2,1)S(1)} %get-tuple-element.8), channel_id=1, source_target_pairs={{1,0},{2,1},{3,2},{4,3},{5,4},{6,5},{7,6},{0,7},{9,8},{10,9},{11,1... | collective-permute-start | bytes 4718600 | tf_op jit(solution)/shard_map/ppermute | solution.py:18
  41.1 0.7 pad_convert_fusion
  42.4 2.1 fusion.10
  44.5 27.2 %collective-permute-done.2 = bf16[3,32,16,4,128]{4,1,3,2,0:T(8,128)(2,1)S(1)} collective-permute-done((bf16[3,32,16,4,128]{4,1,3,2,0:T(8,128)(2,1)S(1)}, bf16[3,32,16,4,128]{4,1,3,2,0:T(8,128)(2,1)S(1)}, u32[]{:S(2)}, u32[]{:S(2)}) %collective-permute-start.2) | collective-permute-done | bytes 1572896 | tf_op jit(solution)/shard_map/ppermute | solution.py:16
  71.7 0.9 collective-permute-done.3
  72.9 2.1 fusion.27
  75.0 2.2 fusion.46
  77.3 3.4 %fusion.4 = f32[32,32]{1,0:T(8,128)} fusion(f32[1,32,8,8,128]{4,1,3,2,0:T(8,128)S(1)} %fusion.10, f32[1,32,8,8,128]{4,1,3,2,0:T(8,128)S(1)} %fusion.27, f32[1,32,8,8,128]{4,1,3,2,0:T(8,128)S(1)} %fusion.46, f32[8,8,128]{2,1,0:T(8,128)S(1)} %copy-done.1), kind=kOutput, calls=%fused_computation.6 | convolution fusion | flops 305922048 | bytes 3182592 | tf_op jit(solution)/shard_map/dot_general | solution.py:56
  80.7 129.6 %all-gather.3.cloned.1.call-done = f32[16384,32]{1,0:T(8,128)} async-done(((f32[32,32]{1,0:T(8,128)}), f32[16384,32]{1,0:T(8,128)}) %all-gather.3.cloned.1.call-update) | async-done | bytes 2097168 | tf_op jit(solution)/shard_map/all_gather | solution.py:63
  210.3 4.0 %reduce_sum.9 = f32[32,32]{1,0:T(8,128)S(1)} reduce(f32[512,32,32]{2,1,0:T(8,128)} %bitcast.51, f32[]{:T(128)} %constant.53.clone.1), dimensions={0}, to_apply=%region_0.1 | reduce | flops 523264 | bytes 2101252 | tf_op jit(solution)/shard_map/reduce_sum | solution.py:63
  214.4 2.9 %cholesky.17 = f32[32,32]{1,0:T(8,128)S(1)} custom-call(f32[32,32]{1,0:T(8,128)S(1)} %fusion.62), custom_call_target="Cholesky" | custom-call | tf_op jit(solution)/shard_map/jit(cholesky)/cholesky | solution.py:63
  217.3 0.6 compare_reduce_fusion
  218.0 0.7 fusion.60
  218.6 2.4 %custom-call.7 = f32[1,32,32]{1,2,0:T(8,128)S(1)} custom-call(f32[1,32,32]{2,1,0:T(8,128)S(1)} %fusion.60), custom_call_target="InvertDiagBlocksLowerTriangular" | custom-call | tf_op jit(solution)/shard_map/jit(_solve_triangular)/triangular_solve | solution.py:64
  221.3 3.0 %multiply_bitcast_fusion = f32[3,32,8,8,128]{4,1,3,2,0:T(8,128)S(1)} fusion(f32[32,32,1,1,1]{1,0,4,3,2:T(8,128)S(1)} %convolution_bitcast_fusion, f32[1,32,8,8,128]{4,1,3,2,0:T(8,128)S(1)} %fusion.10, f32[1,32,8,8,128]{4,1,3,2,0:T(8,128)S(1)} %fusion.27, f32[1,32,8,8,128]{4,1,3,2,0:T(8,128)S(1)} %fusion.46), kind=kOutput, calls=%fused_computation.3 | convolution fusion | flops 304349184 | bytes 6295552 | tf_op jit(solution)/shard_map/ij,cjxzy->cixzy/dot_general | solution.py:69
  224.3 3.5 %copy.16 = f32[3,32,8,8,128]{4,3,2,1,0:T(8,128)} copy(f32[3,32,8,8,128]{4,1,3,2,0:T(8,128)S(1)} %multiply_bitcast_fusion) | data formatting | bytes 6291456 | tf_op jit(solution)/shard_map/mul | solution.py:70
  (16 shorter events, 1.8 us)
Async XLA Ops:
  6.5 203.8 %all-gather.3.cloned.1.call-start = ((), (), s32[]{:S(2)}) async-start(), calls=%async_computation | async-start | bytes 8404992 | tf_op jit(solution)/shard_map/all_gather | solution.py:63
  9.0 14.0 %copy-start = (bf16[3,32,8,8,128]{4,3,2,1,0:T(8,128)(2,1)S(1)}, bf16[3,32,8,8,128]{4,3,2,1,0:T(8,128)(2,1)}, u32[]{:S(2)}) copy-start(bf16[3,32,8,8,128]{4,3,2,1,0:T(8,128)(2,1)} %param.2) | copy-start | bytes 4718596
  9.3 13.6 %collective-permute-start = (bf16[3,32,4,8,128]{4,1,3,2,0:T(8,128)(2,1)S(1)}, bf16[3,32,4,8,128]{4,1,3,2,0:T(8,128)(2,1)S(1)}, u32[]{:S(2)}, u32[]{:S(2)}) collective-permute-start(bf16[3,32,4,8,128]{4,1,3,2,0:T(8,128)(2,1)S(1)} %get-tuple-element.14), channel_id=1, source_target_pairs={{0,8},{8,16},{16,24},{24,32},{32,40},{40,48},{48,56},{56,64},{64,7... | collective-permute-start | bytes 2359304 | tf_op jit(solution)/shard_map/ppermute | solution.py:16
  14.0 13.6 %collective-permute-start.1 = (bf16[3,32,4,8,128]{4,1,3,2,0:T(8,128)(2,1)S(1)}, bf16[3,32,4,8,128]{4,1,3,2,0:T(8,128)(2,1)S(1)}, u32[]{:S(2)}, u32[]{:S(2)}) collective-permute-start(bf16[3,32,4,8,128]{4,1,3,2,0:T(8,128)(2,1)S(1)} %get-tuple-element.13), channel_id=1, source_target_pairs={{8,0},{16,8},{24,16},{32,24},{40,32},{48,40},{56,48},{64,56},{72,6... | collective-permute-start | bytes 2359304 | tf_op jit(solution)/shard_map/ppermute | solution.py:18
  28.7 43.0 %collective-permute-start.2 = (bf16[3,32,16,4,128]{4,1,3,2,0:T(8,128)(2,1)S(1)}, bf16[3,32,16,4,128]{4,1,3,2,0:T(8,128)(2,1)S(1)}, u32[]{:S(2)}, u32[]{:S(2)}) collective-permute-start(bf16[3,32,16,4,128]{4,1,3,2,0:T(8,128)(2,1)S(1)} %get-tuple-element.7), channel_id=1, source_target_pairs={{0,1},{1,2},{2,3},{3,4},{4,5},{5,6},{6,7},{7,0},{8,9},{9,10},{10,1... | collective-permute-start | bytes 4718600 | tf_op jit(solution)/shard_map/ppermute | solution.py:16
  32.4 40.1 %collective-permute-start.3 = (bf16[3,32,16,4,128]{4,1,3,2,0:T(8,128)(2,1)S(1)}, bf16[3,32,16,4,128]{4,1,3,2,0:T(8,128)(2,1)S(1)}, u32[]{:S(2)}, u32[]{:S(2)}) collective-permute-start(bf16[3,32,16,4,128]{4,1,3,2,0:T(8,128)(2,1)S(1)} %get-tuple-element.8), channel_id=1, source_target_pairs={{1,0},{2,1},{3,2},{4,3},{5,4},{6,5},{7,6},{0,7},{9,8},{10,9},{11,1... | collective-permute-start | bytes 4718600 | tf_op jit(solution)/shard_map/ppermute | solution.py:18
  75.0 2.3 copy-start.1
Sparse Core Ops, SparseCore 0:
  80.8 129.4 all-gather.2
